TPU v7x, 32 devices: a whole 2x2x4 slice. The times are simulated.
32 devices in a mesh: scen: 8 (over z, y), rows: 2 (over x), section: 2 (over core).
Axes of the slice: x: 2, y: 2, z: 4, core: 2. Of those that a mesh axis runs over, the one named last changes fastest.
Arguments:
- lp_blocks: bfloat16 [192, 2, 4, 2, 128, 128], P('scen', 'rows', 'section'), may hold values from -0.1875 to 0.1875
- block_columns: int32 [192, 2, 4, 2], P('scen', None, 'section'), may hold values from 0 to 175
- scenario_nodes: int32 [3, 192], P(None, 'scen'), may hold values from 0 to 511, as said below
- scenario_weights: float32 [192], P('scen'), may hold values from 0.5 to 4.5
- cost: bfloat16 [192, 4, 22528], P('scen', 'section'), may hold values from -6 to 6
- bounds_rhs: float32 [192, 256], P('scen', 'rows'), may hold values from -6 to 6
- primal_start: bfloat16 [192, 4, 22528], P('scen', 'section'), may hold values from 0 to 2
- dual_start: float32 [192, 256], P('scen', 'rows'), may hold values from 0 to 1
- multiplier_start: float32 [192, 4, 512], P('scen', 'section'), may hold values from -3 to 3
- consensus_start: float32 [585, 512], replicated, may hold values from 0 to 2
Outputs:
- primal: float32 [192, 4, 22528], P('scen', 'section')
- dual: float32 [192, 256], P('scen', 'rows')
- multiplier: float32 [192, 4, 512], P('scen', 'section')
- penalty: float32 [], replicated
Inputs may be any that keep to these rules, and one draw needn't show every extreme that they name: `scenario_nodes`: node ids never fall from one scenario to the next at any section; the section-three node is the section-four node // 8 and the section-two node the section-three node // 8; the first scenario lies in node 0 and the last in node 511 of section four.
All inputs are finite; a program needn't handle non-finite values.
Results may differ from a plain program's by a relative error of at most 0.0018.
Values sent between devices are 32-bit elements; how exact they have to be, the bound alone decides.
No kernel may reach another device: no remote copies, remote signals or barrier semaphores. Data moves between devices by JAX's collectives and lax.ppermute only.
A program may use at most 128 MiB of HBM per device.

v0:
```python
import jax
import jax.numpy as jnp
from jax import lax
from jax.sharding import PartitionSpec as P

BLK = 128
CPS = 176
N1 = 8
SWEEPS = 2
N2 = 64
NODES = 585
TAU_STEP = 0.4
SIGMA_STEP = 0.4
RHO_START = 1.0
EPSILON = 1e-06


def averaged(node_table, node_mass):
    positive = node_mass > 0
    safe_mass = jnp.where(positive, node_mass, 1.0)
    return jnp.where(positive[:, None], node_table / safe_mass[:, None], 0.0)


def local(
    lp_blocks,
    block_columns,
    scenario_nodes,
    scenario_weights,
    cost,
    bounds_rhs,
    primal_start,
    dual_start,
    multiplier_start,
    consensus_start,
):
    scenario_count = cost.shape[0]
    local_sections = cost.shape[1]
    columns = cost.shape[2]
    hedged = multiplier_start.shape[2]
    row_blocks = dual_start.shape[1] // BLK
    section_index = lax.axis_index("section")
    row_index = lax.axis_index("rows")
    selector = (block_columns[..., None] == jnp.arange(CPS, dtype=jnp.int32)).astype(jnp.float32)
    local_selector = lax.dynamic_slice_in_dim(
        selector, row_index * row_blocks, row_blocks, 1
    ).astype(jnp.bfloat16)
    offsets = jnp.array([1, 1 + N1, 1 + N1 + N2], jnp.int32)
    node_rows = jnp.concatenate(
        [jnp.zeros((1, scenario_count), jnp.int32), scenario_nodes + offsets[:, None]], axis=0
    )
    local_rows = lax.dynamic_slice_in_dim(
        node_rows, section_index * local_sections, local_sections, 0
    )
    membership = (
        local_rows[:, None, :] == jnp.arange(NODES, dtype=jnp.int32)[None, :, None]
    ).astype(jnp.float32)
    cost_full = cost.astype(jnp.float32)

    def spread(table):
        return jnp.einsum("jns,nc->sjc", membership, table, precision=lax.Precision.HIGHEST)

    penalty = jnp.asarray(RHO_START, jnp.float32)
    primal = primal_start.astype(jnp.float32)
    dual, multiplier, previous = (dual_start, multiplier_start, consensus_start)
    for sweep_index in range(SWEEPS):
        anchors = spread(previous)
        dual_half = dual.reshape(scenario_count, row_blocks, BLK).astype(jnp.bfloat16)
        pieces = jnp.einsum(
            "srjnab,sra->srjnb", lp_blocks, dual_half, preferred_element_type=jnp.float32
        )
        gathered = lax.all_gather(pieces, "rows", axis=1, tiled=True)
        placed = jnp.einsum(
            "srjnc,srjnb->sjcb", selector, gathered, precision=lax.Precision.HIGHEST
        )
        adjoint = placed.reshape(scenario_count, local_sections, columns)
        hedge_term = multiplier + penalty * (primal[:, :, :hedged] - anchors)
        hedge_full = jnp.pad(hedge_term, ((0, 0), (0, 0), (0, columns - hedged)))
        primal_next = jnp.maximum(primal - TAU_STEP * (cost_full + adjoint + hedge_full), 0.0)
        step_half = (2.0 * primal_next - primal).astype(jnp.bfloat16)
        blocks = step_half.reshape(scenario_count, local_sections, CPS, BLK)
        picked = jnp.einsum(
            "srjnc,sjcb->srjnb", local_selector, blocks, preferred_element_type=jnp.float32
        ).astype(jnp.bfloat16)
        image = lax.psum(
            jnp.einsum("srjnab,srjnb->sra", lp_blocks, picked, preferred_element_type=jnp.float32),
            "section",
        )
        dual_next = jnp.maximum(
            dual + SIGMA_STEP * (image.reshape(scenario_count, -1) - bounds_rhs), 0.0
        )
        hedged_next = primal_next[:, :, :hedged]
        weighted = scenario_weights[:, None, None] * hedged_next
        node_table, node_mass = lax.psum(
            (
                jnp.einsum("jns,sjc->nc", membership, weighted, precision=lax.Precision.HIGHEST),
                jnp.einsum(
                    "jns,s->n", membership, scenario_weights, precision=lax.Precision.HIGHEST
                ),
            ),
            "scen",
        )
        consensus = averaged(node_table, node_mass)
        new_anchors = spread(consensus)
        gap_local = jnp.sum(scenario_weights[:, None, None] * (hedged_next - new_anchors) ** 2)
        drift_local = jnp.sum(scenario_weights[:, None, None] * (new_anchors - anchors) ** 2)
        primal_gap, drift_gap = lax.psum((gap_local, drift_local), ("scen", "section"))
        multiplier = multiplier + penalty * (hedged_next - new_anchors)
        penalty = penalty * jnp.sqrt(primal_gap / (drift_gap + EPSILON))
        primal, dual, previous = (primal_next, dual_next, consensus)
    return (primal, dual, multiplier, penalty)


def solution(mesh):
    in_specs = (
        P("scen", "rows", "section", None, None, None),
        P("scen", None, "section", None),
        P(None, "scen"),
        P("scen"),
        P("scen", "section", None),
        P("scen", "rows"),
        P("scen", "section", None),
        P("scen", "rows"),
        P("scen", "section", None),
        P(),
    )
    out_specs = (P("scen", "section", None), P("scen", "rows"), P("scen", "section", None), P())
    return jax.shard_map(local, mesh=mesh, in_specs=in_specs, out_specs=out_specs, check_vma=False)
```

profile of v0, /device:TPU:0, one launch (start us, length us, event | category | flops | bytes accessed | tf_op | source)
XLA Modules:
  0.0 297.4 jit_solution(1320190035164285401)
XLA Ops:
  7.2 0.0 copy-start
  7.2 0.0 copy-start.12
  7.2 0.0 all-reduce.8.cloned.1.call-start
  7.2 0.9 convert_bitcast_fusion.1
  8.1 1.0 copy-done
  9.1 0.5 fusion.14
  9.6 0.0 copy-done.12
  9.6 0.1 copy.45
  9.7 5.7 %all-gather = f32[24,4,2,128]{3,0,2,1:T(8,128)S(1)} all-gather(f32[24,2,2,128]{3,0,2,1:T(8,128)S(1)} %bitcast.114), channel_id=2, replica_groups=mesh['scen'=8,'rows'=2,'section'=2] {'rows'}, dimensions={1}, use_global_device_ids=true | all-gather | bytes 147456 | tf_op jit(solution)/shard_map/all_gather | solution.py:71
  15.4 3.8 %fusion.53 = f32[24,2,176,128,1]{3,2,1,0,4:T(8,128)S(1)} fusion(f32[24,2,2,2,128]{4,0,3,2,1:T(8,128)S(1)} %bitcast.113, s32[24,2,2,2]{3,2,0,1:T(2,128)S(1)} %copy.45), kind=kOutput, calls=%fused_computation.58 | convolution fusion | flops 51938304 | bytes 4424448 | tf_op jit(solution)/shard_map/srjnc,srjnb->sjcb/dot_general | solution.py:72
  19.2 2.4 copy.119
  21.6 5.4 %reshape.65 = f32[24,2,22528]{2,0,1:T(8,128)} reshape(f32[24,2,176,128]{3,2,0,1:T(8,128)} %bitcast.103) | data formatting | bytes 8650752 | tf_op jit(solution)/shard_map/reshape | solution.py:75
  26.9 4.4 %copy_convert_fusion = f32[24,2,22528]{2,0,1:T(8,128)} fusion(bf16[24,2,22528]{2,1,0:T(2,128)(2,1)} %param.17), kind=kLoop, calls=%fused_computation.26 | loop fusion | flops 1081344 | bytes 6488064 | tf_op jit(solution)/shard_map/convert_element_type | solution.py:63
  31.3 0.0 copy-done.13
  31.3 0.0 copy-done.14
  31.3 0.1 broadcast_add_fusion
  31.4 0.0 copy-done.4
  31.4 1.9 fusion.50
  33.3 0.0 copy-start.10
  33.3 5.4 %subtract_convert_fusion.1 = (bf16[24,2,22528]{2,0,1:T(8,128)(2,1)}, f32[24,2,22528]{2,0,1:T(8,128)S(1)}) fusion(bf16[24,2,22528]{2,1,0:T(2,128)(2,1)} %param.17, f32[24,2,512]{2,0,1:T(8,128)S(1)} %get-tuple-element.29, f32[24,2,22528]{2,0,1:T(8,128)} %reshape.65, bf16[24,2,22528]{2,1,0:T(2,128)(2,1)} %param.15), kind=kLoop, calls=%fused_computation.13 | loop fusion | flops 10813440 | bytes 15237120 | tf_op jit(solution)/shard_map/convert_element_type | solution.py:79
  38.7 2.0 copy-done.1
  40.7 0.0 copy-done.10
  40.7 1.8 convolution_bitcast_fusion.1
  42.5 0.0 all-reduce.8.cloned.1.call-update
  42.5 0.0 all-reduce.10.cloned.1.call-start
  42.6 0.2 iota_compare_fusion
  42.8 0.0 copy-start.6
  42.8 3.3 %copy.72 = bf16[6,8,176,128]{3,2,1,0:T(8,128)(2,1)} copy(bf16[6,8,176,128]{3,1,2,0:T(8,128)(2,1)} %bitcast.106) | data formatting | bytes 4325376
  46.1 2.3 fusion.40
  48.4 0.0 copy-done.6
  48.4 0.9 fusion.12
  49.3 3.3 %psum.66 = f32[24,128]{1,0:T(8,128)S(1)} all-reduce(f32[24,128]{1,0:T(8,128)S(1)} %bitcast.117), channel_id=1, replica_groups=mesh['scen'=8,'rows'=2,'section'=2] {'section'}, use_global_device_ids=true, to_apply=%region_0.1 | all-reduce | flops 3072 | bytes 24576 | tf_op jit(solution)/shard_map/psum | solution.py:84
  52.6 0.0 copy-done.8
  52.6 0.5 fusion.10
  53.2 5.1 %all-gather.1 = f32[24,4,2,128]{3,0,2,1:T(8,128)S(1)} all-gather(f32[24,2,2,128]{3,0,2,1:T(8,128)S(1)} %bitcast.115), channel_id=3, replica_groups=mesh['scen'=8,'rows'=2,'section'=2] {'rows'}, dimensions={1}, use_global_device_ids=true | all-gather | bytes 147456 | tf_op jit(solution)/shard_map/all_gather | solution.py:71
  58.3 3.8 %fusion.51 = f32[24,2,176,128,1]{3,2,1,0,4:T(8,128)S(1)} fusion(f32[24,2,2,2,128]{4,0,3,2,1:T(8,128)S(1)} %bitcast.112, s32[24,2,2,2]{3,2,0,1:T(2,128)S(1)} %copy.45), kind=kOutput, calls=%fused_computation.56 | convolution fusion | flops 51938304 | bytes 4424448 | tf_op jit(solution)/shard_map/srjnc,srjnb->sjcb/dot_general | solution.py:72
  62.1 2.4 copy.118
  64.5 5.4 %reshape.70 = f32[24,2,22528]{2,0,1:T(8,128)} reshape(f32[24,2,176,128]{3,2,0,1:T(8,128)} %bitcast.104) | data formatting | bytes 8650752 | tf_op jit(solution)/shard_map/reshape | solution.py:75
  69.9 0.1 convert_reduce_fusion
  70.0 0.2 convolution_reduce_fusion
  70.2 22.1 %psum.67 = f32[585]{0:T(1024)S(1)} all-reduce(f32[585]{0:T(1024)S(1)} %convolution_reduce_fusion), channel_id=1, replica_groups=mesh['scen'=8,'rows'=2,'section'=2] {'scen'}, use_global_device_ids=true, to_apply=%region_2.3 | all-reduce | flops 585 | bytes 4680 | tf_op jit(solution)/shard_map/psum | solution.py:93
  92.2 0.1 iota_compare_fusion.1
  92.3 33.4 %all-reduce.8.cloned.1.call-done = f32[585,512]{1,0:T(8,128)} async-done(((f32[585,512]{1,0:T(8,128)}), f32[585,512]{1,0:T(8,128)}) %all-reduce.8.cloned.1.call-update) | async-done | bytes 1198096 | tf_op jit(solution)/shard_map/psum | solution.py:93
  125.8 2.1 fusion.25
  127.8 1.6 multiply_reduce_fusion.2
  129.4 31.8 %all-reduce.4 = (f32[]{:T(128)}, f32[]{:T(128)}) all-reduce(f32[]{:T(128)} %get-tuple-element.19, f32[]{:T(128)} %get-tuple-element.18), channel_id=1, replica_groups=mesh['scen'=8,'rows'=2,'section'=2] {'scen','section'}, use_global_device_ids=true, to_apply=%region_5.6 | all-reduce | flops 2 | bytes 16 | tf_op jit(solution)/shard_map/psum | solution.py:106
  162.6 0.9 multiply_add_fusion.1
  163.5 5.7 %subtract_convert_fusion = (bf16[24,2,22528]{2,0,1:T(8,128)(2,1)}, f32[24,2,22528]{2,0,1:T(8,128)S(1)}) fusion(f32[24,2,22528]{2,0,1:T(8,128)} %copy-done.1, f32[24,2,512]{2,0,1:T(8,128)S(1)} %multiply_add_fusion.1, f32[24,2,22528]{2,0,1:T(8,128)} %reshape.70, bf16[24,2,22528]{2,1,0:T(2,128)(2,1)} %param.15), kind=kLoop, calls=%fused_computation.12 | loop fusion | flops 9732096 | bytes 17399808 | tf_op jit(solution)/shard_map/convert_element_type | solution.py:79
  169.3 2.0 copy-done.2
  171.3 1.8 convolution_bitcast_fusion
  173.1 0.0 all-reduce.10.cloned.1.call-update
  173.1 7.8 %copy.54 = f32[24,2,22528]{2,1,0:T(2,128)} copy(f32[24,2,22528]{2,0,1:T(8,128)} %copy-done.2) | data formatting | bytes 8650752
  180.9 0.0 copy-done.3
  180.9 0.3 copy.73
  181.2 0.6 copy-done.7
  181.8 0.7 fusion.37
  182.5 0.9 fusion.8
  183.4 3.3 %psum.71 = f32[24,128]{1,0:T(8,128)S(1)} all-reduce(f32[24,128]{1,0:T(8,128)S(1)} %bitcast.118), channel_id=1, replica_groups=mesh['scen'=8,'rows'=2,'section'=2] {'section'}, use_global_device_ids=true, to_apply=%region_8.9 | all-reduce | flops 3072 | bytes 24576 | tf_op jit(solution)/shard_map/psum | solution.py:84
  186.7 0.6 add_maximum_fusion
  187.3 64.4 %all-reduce.10.cloned.1.call-done = f32[585,512]{1,0:T(8,128)} async-done(((f32[585,512]{1,0:T(8,128)}), f32[585,512]{1,0:T(8,128)}) %all-reduce.10.cloned.1.call-update) | async-done | bytes 1198096 | tf_op jit(solution)/shard_map/psum | solution.py:93
  251.7 2.1 fusion.22
  253.8 1.7 multiply_reduce_fusion
  255.5 0.7 copy.55
  256.2 31.9 %all-reduce.3 = (f32[]{:T(128)}, f32[]{:T(128)}) all-reduce(f32[]{:T(128)} %get-tuple-element.17, f32[]{:T(128)} %get-tuple-element.16), channel_id=1, replica_groups=mesh['scen'=8,'rows'=2,'section'=2] {'scen','section'}, use_global_device_ids=true, to_apply=%region_11.12 | all-reduce | flops 2 | bytes 16 | tf_op jit(solution)/shard_map/psum | solution.py:106
  (20 shorter events, 0.1 us)
Async XLA Ops:
  7.2 1.9 copy-start
  7.2 2.4 copy-start.12
  7.2 118.6 %all-reduce.8.cloned.1.call-start = ((), (), s32[]{:S(2)}) async-start(), calls=%async_computation | async-start | bytes 2424832 | tf_op jit(solution)/shard_map/psum | solution.py:93
  26.9 4.4 %copy-start.13 = (s32[3,24]{1,0:T(4,128)S(1)}, s32[3,24]{1,0:T(4,128)}, u32[]{:S(2)}) copy-start(s32[3,24]{1,0:T(4,128)} %param.13) | copy-start | bytes 868
  26.9 4.4 %copy-start.14 = (s32[3]{0:T(128)S(1)}, s32[3]{0:T(128)}, u32[]{:S(2)}) copy-start(s32[3]{0:T(128)} %constant.8.clone) | copy-start | bytes 40
  26.9 4.5 %copy-start.4 = (f32[24,2,512]{2,1,0:T(2,128)S(1)}, f32[24,2,512]{2,1,0:T(2,128)}, u32[]{:S(2)}) copy-start(f32[24,2,512]{2,1,0:T(2,128)} %param.19) | copy-start | bytes 294916
  33.3 7.4 %copy-start.10 = (f32[24]{0:T(128)S(1)}, f32[24]{0:T(128)}, u32[]{:S(2)}) copy-start(f32[24]{0:T(128)} %param.14) | copy-start | bytes 292
  38.7 2.0 copy-start.1
  42.5 209.2 %all-reduce.10.cloned.1.call-start = ((), (), s32[]{:S(2)}) async-start(), calls=%async_computation.1 | async-start | bytes 2424832 | tf_op jit(solution)/shard_map/psum | solution.py:93
  42.8 5.6 %copy-start.6 = (pred[24,2,2,2,176]{4,3,2,0,1:T(4,128)(4,1)}, pred[24,2,2,2,176]{4,3,2,0,1:T(4,128)(4,1)S(1)}, u32[]{:S(2)}) copy-start(pred[24,2,2,2,176]{4,3,2,0,1:T(4,128)(4,1)S(1)} %iota_compare_fusion) | copy-start | bytes 101380
  46.1 6.5 %copy-start.5 = (f32[24,128]{1,0:T(8,128)S(1)}, f32[24,128]{1,0:T(8,128)}, u32[]{:S(2)}) copy-start(f32[24,128]{1,0:T(8,128)} %param.18) | copy-start | bytes 36868
  46.1 6.5 %copy-start.8 = (f32[24,128]{1,0:T(8,128)S(1)}, f32[24,128]{1,0:T(8,128)}, u32[]{:S(2)}) copy-start(f32[24,128]{1,0:T(8,128)} %param.16) | copy-start | bytes 36868
  64.5 5.5 %copy-start.11 = (f32[24]{0:T(128)S(1)}, f32[24]{0:T(128)}, u32[]{:S(2)}) copy-start(f32[24]{0:T(128)} %param.14) | copy-start | bytes 292
  169.3 2.0 copy-start.2
  173.1 7.8 %copy-start.3 = (bf16[24,2,22528]{2,0,1:T(8,128)(2,1)S(1)}, bf16[24,2,22528]{2,0,1:T(8,128)(2,1)}, u32[]{:S(2)}) copy-start(bf16[24,2,22528]{2,0,1:T(8,128)(2,1)} %get-tuple-element.24) | copy-start | bytes 6488068
  180.9 0.9 copy-start.7
  181.8 4.9 %copy-start.9 = (f32[24,128]{1,0:T(8,128)S(1)}, f32[24,128]{1,0:T(8,128)}, u32[]{:S(2)}) copy-start(f32[24,128]{1,0:T(8,128)} %param.16) | copy-start | bytes 36868
Sparse Core Ops, SparseCore 0:
  42.7 83.0 all-reduce.7
  173.3 78.4 all-reduce.9
where the time goes:
time: 298 us; the launch traced here: 297 us
  blocking collectives  103 us (35%)
  waiting for transfers between devices  97.9 us (33%)
  local copies, waits for them, and re-layouts  33.3 us (11%)
  matrix products  23.3 us (8%)
  other arithmetic  21.6 us (7%)
  between operations  18.1 us (6%)
    psum x2, waiting for transfers between devices, local(): lax.psum((jnp.einsum('jns,sjc->nc', membership, weighted, precision=lax.P...  97.8 us
    psum x2, blocking collectives, local(): lax.psum((gap_local, drift_local), ('scen', 'section'))  63.7 us
    psum x1, blocking collectives, local(): lax.psum((jnp.einsum('jns,sjc->nc', membership, weighted, precision=lax.P...  22.1 us
    unnamed x35, local copies, waits for them, and re-layouts  17.8 us
    convert_element_type x2, other arithmetic, local(): step_half = (2.0 * primal_next - primal).astype(jnp.bfloat16)  11.1 us
    reshape x2, local copies, waits for them, and re-layouts, local(): adjoint = placed.reshape(scenario_count, local_sections, columns)  10.8 us
    all_gather x2, blocking collectives, local(): gathered = lax.all_gather(pieces, 'rows', axis=1, tiled=True)  10.8 us
    dot_general x2, matrix products, local(): jnp.einsum('srjnc,srjnb->sjcb', selector, gathered, precision=lax.Precisi...  7.67 us
  transfers between devices with their start and end apart: 2, of which 2 were waited for; matrix products, arithmetic and copies ran while one was open for 10% of the time, Pallas kernels for 0%

commit v1 on v0

--- a/solution.py
+++ b/solution.py
@@ -2,6 +2,7 @@
 import jax.numpy as jnp
 from jax import lax
 from jax.sharding import PartitionSpec as P
+from jax.lax import axis_index, ppermute, psum
 
 BLK = 128
 CPS = 176
@@ -68,10 +69,26 @@
         pieces = jnp.einsum(
             "srjnab,sra->srjnb", lp_blocks, dual_half, preferred_element_type=jnp.float32
         )
-        gathered = lax.all_gather(pieces, "rows", axis=1, tiled=True)
+        block_out, step_out = (psum(1, "rows"), axis_index("rows"))
+        buffer = [(num, (num - 1) % block_out) for num in range(block_out)]
+        value_now = pieces
+        a_now = pieces.shape[1]
         placed = jnp.einsum(
-            "srjnc,srjnb->sjcb", selector, gathered, precision=lax.Precision.HIGHEST
+            "srjnc,srjnb->sjcb",
+            lax.dynamic_slice_in_dim(selector, step_out * a_now, value_now.shape[1], axis=1),
+            value_now,
+            precision=lax.Precision.HIGHEST,
         )
+        for c in range(1, block_out):
+            value_now = ppermute(value_now, "rows", buffer)
+            placed = placed + jnp.einsum(
+                "srjnc,srjnb->sjcb",
+                lax.dynamic_slice_in_dim(
+                    selector, (step_out + c) % block_out * a_now, value_now.shape[1], axis=1
+                ),
+                value_now,
+                precision=lax.Precision.HIGHEST,
+            )
         adjoint = placed.reshape(scenario_count, local_sections, columns)
         hedge_term = multiplier + penalty * (primal[:, :, :hedged] - anchors)
         hedge_full = jnp.pad(hedge_term, ((0, 0), (0, 0), (0, columns - hedged)))

time: 298 us -> 331 us (1.11)
  waiting for transfers between devices: 97.9 us -> 125 us
  matrix products: 23.3 us -> 39.2 us
  blocking collectives: 103 us -> 92 us
  local copies, waits for them, and re-layouts: 33.3 us -> 25.6 us
  other arithmetic: 21.6 us -> 26.4 us
  starting transfers between devices: 0.08 us -> 3.59 us
    psum x2, waiting for transfers between devices: 97.8 us -> 125 us  [local(): lax.psum((jnp.einsum('jns,sjc->nc', membership, weighted, precision=lax.P...]
    dot_general x2 -> x4, matrix products: 7.67 us -> 24.1 us  [the longest x2 13.7 us: local(): jnp.einsum('srjnc,srjnb->sjcb', lax.dynamic_slice_in_dim(selector, (step_...]
    all_gather x2 -> x0, blocking collectives: 10.8 us -> none  [local(): gathered = lax.all_gather(pieces, 'rows', axis=1, tiled=True)]
    unnamed x35 -> x45, local copies, waits for them, and re-layouts: 17.8 us -> 12.2 us
    dot_general x4 -> x0, local copies, waits for them, and re-layouts: 4.73 us -> none  [the longest x2 4.72 us: local(): jnp.einsum('srjnc,srjnb->sjcb', selector, gathered, precision=lax.Precisi...]
    ppermute x0 -> x2, starting transfers between devices: none -> 3.51 us  [local(): value_now = ppermute(value_now, 'rows', buffer)]
  transfers between devices with their start and end apart: 2 -> 4, of which waited for: 2 -> 2; matrix products, arithmetic and copies ran while one was open for 10% -> 13% of each run, Pallas kernels for 0% -> 0%
where the time goes in v1:
time: 331 us; the launch traced here: 330 us
  waiting for transfers between devices  125 us (38%)
  blocking collectives  92 us (28%)
  matrix products  39.2 us (12%)
  other arithmetic  26.4 us (8%)
  local copies, waits for them, and re-layouts  25.6 us (8%)
  between operations  18.2 us (5%)
  starting transfers between devices  3.59 us (1%)
    psum x2, waiting for transfers between devices, local(): lax.psum((jnp.einsum('jns,sjc->nc', membership, weighted, precision=lax.P...  125 us
    psum x2, blocking collectives, local(): lax.psum((gap_local, drift_local), ('scen', 'section'))  63.7 us
    psum x1, blocking collectives, local(): lax.psum((jnp.einsum('jns,sjc->nc', membership, weighted, precision=lax.P...  21.7 us
    convert_element_type x2, other arithmetic, local(): step_half = (2.0 * primal_next - primal).astype(jnp.bfloat16)  14.3 us
    dot_general x2, matrix products, local(): jnp.einsum('srjnc,srjnb->sjcb', lax.dynamic_slice_in_dim(selector, (step_...  13.7 us
    reshape x2, local copies, waits for them, and re-layouts, local(): adjoint = placed.reshape(scenario_count, local_sections, columns)  13.4 us
    unnamed x45, local copies, waits for them, and re-layouts  12.2 us
    dot_general x2, matrix products, local(): jnp.einsum('srjnc,srjnb->sjcb', lax.dynamic_slice_in_dim(selector, step_o...  10.4 us
  transfers between devices with their start and end apart: 4, of which 2 were waited for; matrix products, arithmetic and copies ran while one was open for 13% of the time, Pallas kernels for 0%

profile of v1, /device:TPU:0, one launch (start us, length us, event | category | flops | bytes accessed | tf_op | source)
XLA Modules:
  0.0 330.5 jit_solution(9752587330020329745)
XLA Ops:
  7.2 0.0 copy-start
  7.2 0.0 copy-start.19
  7.2 0.0 copy-start.11
  7.2 0.0 all-reduce.8.cloned.1.call-start
  7.3 0.9 convert_bitcast_fusion.1
  8.1 0.9 copy-done
  9.1 1.1 fusion.14
  10.2 2.9 collective-permute-start
  13.2 0.0 copy-done.17
  13.2 0.1 broadcast_add_fusion
  13.2 0.7 iota_compare_fusion.1
  13.9 0.1 convert_reduce_fusion
  14.0 0.0 copy-done.16
  14.0 0.1 copy.28
  14.1 0.2 iota_compare_fusion
  14.3 0.2 convolution_reduce_fusion
  14.5 21.7 %psum.67 = f32[585]{0:T(1024)S(1)} all-reduce(f32[585]{0:T(1024)S(1)} %convolution_reduce_fusion), channel_id=1, replica_groups=mesh['scen'=8,'rows'=2,'section'=2] {'scen'}, use_global_device_ids=true, to_apply=%region_2.3 | all-reduce | flops 585 | bytes 4680 | tf_op jit(solution)/shard_map/psum | solution.py:110
  36.2 0.6 broadcast_select_fusion
  36.8 4.4 %copy_convert_fusion = f32[24,2,22528]{2,0,1:T(8,128)} fusion(bf16[24,2,22528]{2,1,0:T(2,128)(2,1)} %param.17), kind=kLoop, calls=%fused_computation.26 | loop fusion | flops 1081344 | bytes 6488064 | tf_op jit(solution)/shard_map/convert_element_type | solution.py:64
  41.2 6.6 %fusion.53 = f32[24,2,176,128]{3,2,1,0:T(8,128)} fusion(f32[24,2,2,128]{3,2,1,0:T(2,128)} %bitcast.4, pred[24,2,2,2,176]{4,3,2,0,1:T(4,128)(4,1)S(1)} %iota_compare_fusion, s32[]{:T(128)S(6)} %select_n.33), kind=kOutput, calls=%fused_computation.54 | convolution fusion | flops 25952256 | bytes 4423684 | tf_op jit(solution)/shard_map/srjnc,srjnb->sjcb/dot_general | solution.py:76
  47.8 1.5 fusion.57
  49.3 0.5 broadcast_compare_fusion
  49.8 0.0 collective-permute-done
  49.8 8.1 %convolution_add_fusion.1 = f32[24,2,176,128]{3,2,1,0:T(8,128)} fusion(f32[24,2,176,128]{3,2,1,0:T(8,128)} %fusion.53, pred[24,2,2,2,176]{4,3,2,0,1:T(4,128)(4,1)S(1)} %iota_compare_fusion, s32[]{:T(128)S(6)} %select_n.35, f32[24,1,2,2,128]{4,3,2,0,1:T(2,128)} %collective-permute-done), kind=kOutput, calls=%fused_computation.21 | convolution fusion | flops 27033600 | bytes 8749060 | tf_op jit(solution)/shard_map/srjnc,srjnb->sjcb/dot_general | solution.py:84
  57.9 6.7 %reshape.86 = f32[24,2,22528]{2,1,0:T(2,128)} reshape(f32[24,2,176,128]{3,2,1,0:T(8,128)} %convolution_add_fusion.1) | data formatting | bytes 8650752 | tf_op jit(solution)/shard_map/reshape | solution.py:92
  64.6 7.5 %subtract_convert_fusion.1 = (bf16[24,2,22528]{2,0,1:T(8,128)(2,1)S(1)}, f32[24,2,22528]{2,0,1:T(8,128)}) fusion(bf16[24,2,22528]{2,1,0:T(2,128)(2,1)} %param.17, f32[24,2,512]{2,0,1:T(8,128)S(1)} %get-tuple-element.25, f32[24,2,22528]{2,1,0:T(2,128)} %reshape.86, bf16[24,2,22528]{2,1,0:T(2,128)(2,1)} %param.15), kind=kLoop, calls=%fused_computation.11 | loop fusion | flops 10813440 | bytes 15237120 | tf_op jit(solution)/shard_map/convert_element_type | solution.py:96
  72.1 0.3 copy.46
  72.4 0.0 copy-start.12
  72.4 0.7 fusion.40
  73.1 0.9 fusion.12
  74.0 3.3 psum.66
  77.3 0.0 copy-done.12
  77.3 2.7 convolution_bitcast_fusion.1
  80.0 0.0 all-reduce.8.cloned.1.call-update
  80.0 0.0 all-reduce.10.cloned.1.call-start
  80.1 0.5 fusion.10
  80.6 0.6 collective-permute-start.1
  81.2 3.8 %fusion.51 = f32[24,2,176,128]{3,2,1,0:T(8,128)S(1)} fusion(f32[24,2,2,128]{3,2,1,0:T(2,128)S(1)} %bitcast.117, pred[24,2,2,2,176]{4,3,2,0,1:T(4,128)(4,1)S(1)} %iota_compare_fusion, s32[]{:T(128)S(6)} %select_n.33), kind=kOutput, calls=%fused_computation.52 | convolution fusion | flops 25952256 | bytes 4423684 | tf_op jit(solution)/shard_map/srjnc,srjnb->sjcb/dot_general | solution.py:76
  85.0 0.0 collective-permute-done.1
  85.0 5.6 %convolution_add_fusion = f32[24,2,176,128]{3,2,1,0:T(8,128)} fusion(f32[24,2,176,128]{3,2,1,0:T(8,128)S(1)} %fusion.51, pred[24,2,2,2,176]{4,3,2,0,1:T(4,128)(4,1)S(1)} %iota_compare_fusion, s32[]{:T(128)S(6)} %select_n.35, f32[24,1,2,2,128]{4,3,2,0,1:T(2,128)S(1)} %collective-permute-done.1), kind=kOutput, calls=%fused_computation.20 | convolution fusion | flops 27033600 | bytes 8749060 | tf_op jit(solution)/shard_map/srjnc,srjnb->sjcb/dot_general | solution.py:84
  90.6 6.7 %reshape.115 = f32[24,2,22528]{2,1,0:T(2,128)} reshape(f32[24,2,176,128]{3,2,1,0:T(8,128)} %convolution_add_fusion) | data formatting | bytes 8650752 | tf_op jit(solution)/shard_map/reshape | solution.py:92
  97.3 60.4 %all-reduce.8.cloned.1.call-done = f32[585,512]{1,0:T(8,128)} async-done(((f32[585,512]{1,0:T(8,128)}), f32[585,512]{1,0:T(8,128)}) %all-reduce.8.cloned.1.call-update) | async-done | bytes 1198096 | tf_op jit(solution)/shard_map/psum | solution.py:110
  157.7 2.1 fusion.25
  159.8 1.6 multiply_reduce_fusion.2
  161.4 31.8 %all-reduce.4 = (f32[]{:T(128)}, f32[]{:T(128)}) all-reduce(f32[]{:T(128)} %get-tuple-element.15, f32[]{:T(128)} %get-tuple-element.14), channel_id=1, replica_groups=mesh['scen'=8,'rows'=2,'section'=2] {'scen','section'}, use_global_device_ids=true, to_apply=%region_5.6 | all-reduce | flops 2 | bytes 16 | tf_op jit(solution)/shard_map/psum | solution.py:123
  194.6 0.9 multiply_add_fusion.1
  195.5 0.0 copy-start.14
  195.5 6.8 %subtract_convert_fusion = (bf16[24,2,22528]{2,0,1:T(8,128)(2,1)}, f32[24,2,22528]{2,0,1:T(8,128)S(1)}) fusion(f32[24,2,22528]{2,0,1:T(8,128)} %get-tuple-element.23, f32[24,2,512]{2,0,1:T(8,128)S(1)} %multiply_add_fusion.1, f32[24,2,22528]{2,1,0:T(2,128)} %reshape.115, bf16[24,2,22528]{2,1,0:T(2,128)(2,1)} %param.15), kind=kLoop, calls=%fused_computation.10 | loop fusion | flops 9732096 | bytes 17399808 | tf_op jit(solution)/shard_map/convert_element_type | solution.py:96
  202.3 2.0 copy-done.1
  204.3 1.8 convolution_bitcast_fusion
  206.1 0.0 all-reduce.10.cloned.1.call-update
  206.2 7.8 %copy.35 = f32[24,2,22528]{2,1,0:T(2,128)} copy(f32[24,2,22528]{2,0,1:T(8,128)} %copy-done.1) | data formatting | bytes 8650752
  213.9 0.3 copy.47
  214.2 0.0 copy-start.7
  214.2 0.0 copy-start.9
  214.3 0.7 fusion.37
  215.0 0.9 fusion.8
  215.9 3.3 psum.71
  219.2 0.6 add_maximum_fusion
  219.8 65.0 %all-reduce.10.cloned.1.call-done = f32[585,512]{1,0:T(8,128)} async-done(((f32[585,512]{1,0:T(8,128)}), f32[585,512]{1,0:T(8,128)}) %all-reduce.10.cloned.1.call-update) | async-done | bytes 1198096 | tf_op jit(solution)/shard_map/psum | solution.py:110
  284.8 2.1 fusion.22
  286.9 1.7 multiply_reduce_fusion
  288.5 0.7 copy.36
  289.2 31.9 %all-reduce.3 = (f32[]{:T(128)}, f32[]{:T(128)}) all-reduce(f32[]{:T(128)} %get-tuple-element.13, f32[]{:T(128)} %get-tuple-element.12), channel_id=1, replica_groups=mesh['scen'=8,'rows'=2,'section'=2] {'scen','section'}, use_global_device_ids=true, to_apply=%region_11.12 | all-reduce | flops 2 | bytes 16 | tf_op jit(solution)/shard_map/psum | solution.py:123
  (30 shorter events, 0.1 us)
Async XLA Ops:
  7.2 1.9 copy-start
  7.2 6.0 %copy-start.19 = (s32[3]{0:T(128)S(1)}, s32[3]{0:T(128)}, u32[]{:S(2)}) copy-start(s32[3]{0:T(128)} %constant.43.clone) | copy-start | bytes 40
  7.2 6.0 %copy-start.17 = (s32[3,24]{1,0:T(4,128)S(1)}, s32[3,24]{1,0:T(4,128)}, u32[]{:S(2)}) copy-start(s32[3,24]{1,0:T(4,128)} %param.13) | copy-start | bytes 868
  7.2 6.8 %copy-start.16 = (s32[24,2,2,2]{0,3,2,1:T(2,128)S(1)}, s32[24,2,2,2]{0,3,2,1:T(2,128)}, u32[]{:S(2)}) copy-start(s32[24,2,2,2]{0,3,2,1:T(2,128)} %param.12) | copy-start | bytes 2308
  7.2 7.1 %copy-start.11 = (f32[24]{0:T(128)S(1)}, f32[24]{0:T(128)}, u32[]{:S(2)}) copy-start(f32[24]{0:T(128)} %param.14) | copy-start | bytes 292
  7.2 150.5 %all-reduce.8.cloned.1.call-start = ((), (), s32[]{:S(2)}) async-start(), calls=%async_computation | async-start | bytes 2424832 | tf_op jit(solution)/shard_map/psum | solution.py:110
  10.2 39.6 %collective-permute-start = (f32[24,1,2,2,128]{4,3,2,0,1:T(2,128)}, f32[24,1,2,2,128]{4,3,2,0,1:T(2,128)}, u32[]{:S(2)}, u32[]{:S(2)}) collective-permute-start(f32[24,1,2,2,128]{4,3,2,0,1:T(2,128)} %bitcast.6), channel_id=1, source_target_pairs={{0,2},{2,0},{1,3},{3,1},{4,6},{6,4},{5,7},{7,5},{8,10},{10,8},{9,1... | collective-permute-start | bytes 147464 | tf_op jit(solution)/shard_map/ppermute | solution.py:83
  41.2 6.6 %copy-start.4 = (f32[24,2,512]{2,1,0:T(2,128)S(1)}, f32[24,2,512]{2,1,0:T(2,128)}, u32[]{:S(2)}) copy-start(f32[24,2,512]{2,1,0:T(2,128)} %param.19) | copy-start | bytes 294916
  41.2 6.6 %copy-start.3 = (f32[585,512]{1,0:T(8,128)S(1)}, f32[585,512]{1,0:T(8,128)}, u32[]{:S(2)}) copy-start(f32[585,512]{1,0:T(8,128)} %param.20) | copy-start | bytes 3594244
  72.4 4.9 %copy-start.12 = (f32[24]{0:T(128)S(1)}, f32[24]{0:T(128)}, u32[]{:S(2)}) copy-start(f32[24]{0:T(128)} %param.14) | copy-start | bytes 292
  73.1 7.0 %copy-start.5 = (f32[24,128]{1,0:T(8,128)S(1)}, f32[24,128]{1,0:T(8,128)}, u32[]{:S(2)}) copy-start(f32[24,128]{1,0:T(8,128)} %param.18) | copy-start | bytes 36868
  73.1 7.0 %copy-start.8 = (f32[24,128]{1,0:T(8,128)S(1)}, f32[24,128]{1,0:T(8,128)}, u32[]{:S(2)}) copy-start(f32[24,128]{1,0:T(8,128)} %param.16) | copy-start | bytes 36868
  77.3 2.8 copy-start.6
  80.0 204.8 %all-reduce.10.cloned.1.call-start = ((), (), s32[]{:S(2)}) async-start(), calls=%async_computation.1 | async-start | bytes 2424832 | tf_op jit(solution)/shard_map/psum | solution.py:110
  80.6 4.3 %collective-permute-start.1 = (f32[24,1,2,2,128]{4,3,2,0,1:T(2,128)S(1)}, f32[24,1,2,2,128]{4,3,2,0,1:T(2,128)S(1)}, u32[]{:S(2)}, u32[]{:S(2)}) collective-permute-start(f32[24,1,2,2,128]{4,3,2,0,1:T(2,128)S(1)} %bitcast.116), channel_id=1, source_target_pairs={{0,2},{2,0},{1,3},{3,1},{4,6},{6,4},{5,7},{7,5},{8,10},{10,8},{9,1... | collective-permute-start | bytes 147464 | tf_op jit(solution)/shard_map/ppermute | solution.py:83
  157.7 2.1 copy-start.13
  195.5 8.8 %copy-start.14 = (f32[24]{0:T(128)S(1)}, f32[24]{0:T(128)}, u32[]{:S(2)}) copy-start(f32[24]{0:T(128)} %param.14) | copy-start | bytes 292
  202.3 2.0 copy-start.1
  206.1 7.8 %copy-start.2 = (bf16[24,2,22528]{2,0,1:T(8,128)(2,1)S(1)}, bf16[24,2,22528]{2,0,1:T(8,128)(2,1)}, u32[]{:S(2)}) copy-start(bf16[24,2,22528]{2,0,1:T(8,128)(2,1)} %get-tuple-element.20) | copy-start | bytes 6488068
  214.2 4.9 %copy-start.7 = (f32[24,128]{1,0:T(8,128)S(1)}, f32[24,128]{1,0:T(8,128)}, u32[]{:S(2)}) copy-start(f32[24,128]{1,0:T(8,128)} %copy-done.6) | copy-start | bytes 36868
  214.2 4.9 %copy-start.9 = (f32[24,128]{1,0:T(8,128)S(1)}, f32[24,128]{1,0:T(8,128)}, u32[]{:S(2)}) copy-start(f32[24,128]{1,0:T(8,128)} %param.16) | copy-start | bytes 36868
  214.3 70.5 %copy-start.10 = (pred[2,585,24]{1,2,0:T(8,128)(4,1)S(1)}, pred[2,585,24]{1,2,0:T(8,128)(4,1)}, u32[]{:S(2)}) copy-start(pred[2,585,24]{1,2,0:T(8,128)(4,1)} %iota_compare_fusion.1) | copy-start | bytes 84244
  214.3 70.5 %copy-start.15 = (f32[585]{0:T(1024)S(1)}, f32[585]{0:T(1024)}, u32[]{:S(2)}) copy-start(f32[585]{0:T(1024)} %broadcast_select_fusion) | copy-start | bytes 7024
  214.9 69.8 %copy-start.18 = (pred[585]{0:T(1024)(128)(4,1)S(1)}, pred[585]{0:T(1024)(128)(4,1)}, u32[]{:S(2)}) copy-start(pred[585]{0:T(1024)(128)(4,1)} %broadcast_compare_fusion) | copy-start | bytes 1759
Sparse Core Ops, SparseCore 0:
  80.1 77.5 all-reduce.7
  206.3 78.4 all-reduce.9
